TPU v7x, 32 devices: a whole 2x2x4 slice. The times are simulated.
32 devices in a mesh: row: 8 (over z, y), col: 4 (over x, core).
Axes of the slice: x: 2, y: 2, z: 4, core: 2. Of those that a mesh axis runs over, the one named last changes fastest.
Arguments:
- start_block: float32 [64, 16, 128], P(('row', 'col')), may hold values from -6 to 6
- blocks: float32 [8, 4, 58, 128, 128], P('row', 'col'), as said below
- slot_row: int32 [8, 4, 58], P('row', 'col'), may hold values from 0 to 7, as said below
- slot_col: int32 [8, 4, 58], P('row', 'col'), may hold values from 0 to 15, as said below
- counts: int32 [8, 4], P('row', 'col'), may hold values from 34 to 58, as said below
Outputs:
- alphas: float32 [2, 16, 16], replicated
- betas: float32 [2, 16, 16], replicated
- next_block: float32 [64, 16, 128], P(('row', 'col'))
Inputs may be any that keep to these rules, and one draw needn't show every extreme that they name: `blocks`: over all cells the live slots list each nonzero block of a symmetric matrix exactly once: block (J, I) is listed exactly when (I, J) is, holding its transpose. Slots at or past a cell's count hold finite values that are no part of H. `counts`: live slots of a cell come first; in every draw some cell has all 58 slots live. `slot_row`: for live slots, the block row within the cell's row group of 8 block rows. `slot_col`: for live slots, the position within the cell's column group of 16 block columns, as in the first step.
All inputs are finite; a program needn't handle non-finite values.
Results may differ from a plain program's by a relative error of at most 0.0003.
Values sent between devices are 32-bit elements; how exact they have to be, the bound alone decides.
A program may use at most 64 MiB of HBM per device.

v0:
```python
import jax
import jax.numpy as jnp
from jax import lax
from jax.sharding import PartitionSpec as P

ITERS = 2
highest = lax.Precision.HIGHEST


def matmul(left, right):
    return jnp.dot(left, right, precision=highest, preferred_element_type=jnp.float32)


def local_gram(left, right):
    return jnp.einsum(
        "bki,bli->kl", left, right, precision=highest, preferred_element_type=jnp.float32
    )


def on_device(start_block, blocks, slot_row, slot_col, counts):
    matrix_tiles = blocks[0, 0]
    rows_local = slot_row[0, 0]
    cols_local = slot_col[0, 0]
    capacity = matrix_tiles.shape[0]
    active = lax.iota(jnp.int32, capacity) < counts[0, 0]
    piece_rows = start_block.shape[0]
    vec_count = start_block.shape[1]
    orbitals = start_block.shape[2]
    row_total = float(piece_rows * lax.axis_size("row") * lax.axis_size("col") * orbitals)
    identity = jnp.eye(vec_count, dtype=jnp.float32)
    start_mean = lax.psum(local_gram(start_block, start_block), ("row", "col")) / row_total
    factor = jnp.linalg.cholesky(start_mean)
    inverse = jax.scipy.linalg.solve_triangular(factor, identity, lower=True)
    vectors = jnp.einsum(
        "kl,bli->bki", inverse, start_block, precision=highest, preferred_element_type=jnp.float32
    )
    previous = jnp.zeros(vectors.shape, jnp.float32)
    beta_prev = jnp.zeros((vec_count, vec_count), jnp.float32)
    alpha_list = []
    beta_list = []
    for iteration in range(ITERS):
        gathered = lax.all_gather(vectors, "row", axis=0, tiled=True)
        operate_product = jnp.einsum(
            "sij,skj->ski",
            matrix_tiles,
            gathered[cols_local],
            precision=highest,
            preferred_element_type=jnp.float32,
        )
        targets = lax.iota(jnp.int32, lax.axis_size("col") * piece_rows)
        selector = ((rows_local[None, :] == targets[:, None]) & active[None, :]).astype(jnp.float32)
        image_block = lax.psum_scatter(
            jnp.einsum(
                "rs,ski->rki",
                selector,
                operate_product,
                precision=highest,
                preferred_element_type=jnp.float32,
            ),
            "col",
            scatter_dimension=0,
            tiled=True,
        )
        stacked = jnp.concatenate([image_block, vectors, previous], axis=1)
        all_means = lax.psum(local_gram(stacked, stacked), ("row", "col")) / row_total
        yy_mean = all_means[:vec_count, :vec_count]
        vy_mean = all_means[vec_count : 2 * vec_count, :vec_count]
        py_mean = all_means[2 * vec_count :, :vec_count]
        vv_mean = all_means[vec_count : 2 * vec_count, vec_count : 2 * vec_count]
        pv_mean = all_means[2 * vec_count :, vec_count : 2 * vec_count]
        pp_mean = all_means[2 * vec_count :, 2 * vec_count :]
        residual = image_block - jnp.einsum(
            "lk,bli->bki", vy_mean, vectors, precision=highest, preferred_element_type=jnp.float32
        )
        residual = residual - jnp.einsum(
            "kl,bli->bki",
            beta_prev,
            previous,
            precision=highest,
            preferred_element_type=jnp.float32,
        )
        gram_mean = yy_mean - matmul(vy_mean.T, vy_mean) - matmul(vy_mean.T, vy_mean)
        gram_mean = gram_mean + matmul(matmul(vy_mean.T, vv_mean), vy_mean)
        gram_mean = gram_mean - matmul(py_mean.T, beta_prev.T) - matmul(beta_prev, py_mean)
        gram_mean = gram_mean + matmul(matmul(vy_mean.T, pv_mean.T), beta_prev.T)
        gram_mean = gram_mean + matmul(matmul(beta_prev, pv_mean), vy_mean)
        gram_mean = gram_mean + matmul(matmul(beta_prev, pp_mean), beta_prev.T)
        factor = jnp.linalg.cholesky(gram_mean)
        beta_block = factor.T
        inverse = jax.scipy.linalg.solve_triangular(factor, identity, lower=True)
        previous = vectors
        vectors = jnp.einsum(
            "kl,bli->bki", inverse, residual, precision=highest, preferred_element_type=jnp.float32
        )
        beta_prev = beta_block
        alpha_list.append(vy_mean)
        beta_list.append(beta_block)
    return (jnp.stack(alpha_list), jnp.stack(beta_list), vectors)


def solution(mesh):
    placed = (
        P(("row", "col"), None, None),
        P("row", "col", None, None, None),
        P("row", "col", None),
        P("row", "col", None),
        P("row", "col"),
    )
    return jax.shard_map(
        on_device,
        mesh=mesh,
        in_specs=placed,
        out_specs=(P(), P(), P(("row", "col"), None, None)),
        check_vma=False,
    )
```

profile of v0, /device:TPU:0, one launch (start us, length us, event | category | flops | bytes accessed | tf_op | source)
XLA Modules:
  0.0 285.7 jit_solution(17474431526224107313)
XLA Ops:
  8.7 42.0 %psum.21 = f32[16,16]{0,1:T(8,128)S(1)} all-reduce(f32[16,16]{0,1:T(8,128)S(1)} %convolution_bitcast_fusion.12), channel_id=1, replica_groups=mesh['row'=8,'col'=4] {'row','col'}, use_global_device_ids=true, to_apply=%region_0.0 | all-reduce | flops 256 | bytes 2048 | tf_op jit(solution)/shard_map/psum | solution.py:31
  50.8 1.5 cholesky.59
  53.6 1.2 custom-call.7
  55.1 30.6 %all_gather.6 = f32[16,16,128]{2,1,0:T(8,128)S(1)} all-gather(f32[2,16,128]{2,1,0:T(8,128)S(1)} %convolution_bitcast_fusion.8), channel_id=1, replica_groups=mesh['row'=8,'col'=4] {'row'}, dimensions={0}, use_global_device_ids=true | all-gather | bytes 147456 | tf_op jit(solution)/shard_map/all_gather | solution.py:42
  86.4 8.1 %fusion.2 = f32[58,16,128]{2,1,0:T(8,128)S(1)} fusion(f32[58,16,128]{2,1,0:T(8,128)S(1)} %gather_fusion, f32[1,1,58,128,128]{4,3,2,1,0:T(8,128)} %param.9), kind=kOutput, calls=%fused_computation.4 | convolution fusion | flops 182452224 | bytes 4751360 | tf_op jit(solution)/shard_map/sij,skj->ski/dot_general | solution.py:43
  95.6 19.3 %reduce-scatter.3.cloned.1.call-done = f32[2,16,128]{2,1,0:T(8,128)} async-done(((f32[8,16,128]{2,1,0:T(8,128)}), f32[2,16,128]{2,1,0:T(8,128)}) %reduce-scatter.3.cloned.1.call-update) | async-done | bytes 16400 | tf_op jit(solution)/shard_map/reduce_scatter | solution.py:52
  114.9 1.0 convolution_bitcast_fusion.1
  115.9 39.5 %psum.22 = f32[48,48]{0,1:T(8,128)S(1)} all-reduce(f32[48,48]{0,1:T(8,128)S(1)} %convolution_bitcast_fusion.1), channel_id=1, replica_groups=mesh['row'=8,'col'=4] {'row','col'}, use_global_device_ids=true, to_apply=%region_4.0 | all-reduce | flops 2304 | bytes 18432 | tf_op jit(solution)/shard_map/psum | solution.py:65
  156.4 0.9 fusion.7
  158.7 1.5 cholesky.70
  161.5 1.2 custom-call.8
  163.0 30.7 %all_gather.7 = f32[16,16,128]{2,1,0:T(8,128)S(1)} all-gather(f32[2,16,128]{2,1,0:T(8,128)S(1)} %convolution_bitcast_fusion.5), channel_id=1, replica_groups=mesh['row'=8,'col'=4] {'row'}, dimensions={0}, use_global_device_ids=true | all-gather | bytes 147456 | tf_op jit(solution)/shard_map/all_gather | solution.py:42
  194.4 8.1 %fusion = f32[58,16,128]{2,1,0:T(8,128)S(1)} fusion(f32[58,16,128]{2,1,0:T(8,128)S(1)} %gather_fusion.1, f32[1,1,58,128,128]{4,3,2,1,0:T(8,128)} %param.9), kind=kOutput, calls=%fused_computation.2 | convolution fusion | flops 182452224 | bytes 4751360 | tf_op jit(solution)/shard_map/sij,skj->ski/dot_general | solution.py:43
  203.6 20.4 %reduce-scatter.5.cloned.1.call-done = f32[2,16,128]{2,1,0:T(8,128)} async-done(((f32[8,16,128]{2,1,0:T(8,128)}), f32[2,16,128]{2,1,0:T(8,128)}) %reduce-scatter.5.cloned.1.call-update) | async-done | bytes 16400 | tf_op jit(solution)/shard_map/reduce_scatter | solution.py:52
  223.9 1.0 convolution_bitcast_fusion
  224.9 39.5 %psum.23 = f32[48,48]{0,1:T(8,128)S(1)} all-reduce(f32[48,48]{0,1:T(8,128)S(1)} %convolution_bitcast_fusion), channel_id=1, replica_groups=mesh['row'=8,'col'=4] {'row','col'}, use_global_device_ids=true, to_apply=%region_6.9 | all-reduce | flops 2304 | bytes 18432 | tf_op jit(solution)/shard_map/psum | solution.py:65
  265.3 0.9 fusion.26
  266.9 0.9 fusion.5
  267.8 0.8 fusion.4
  268.8 0.9 convolution_subtract_fusion.1
  269.7 0.9 convolution_subtract_fusion
  272.3 0.9 convolution_add_fusion
  273.2 1.5 cholesky.81
  276.0 1.2 custom-call.9
  (68 shorter events, 16.6 us)
Async XLA Ops:
  7.2 1.4 copy-start
  7.2 87.3 %copy-start.1 = (s32[1,1,58]{2,1,0:T(1,128)S(1)}, s32[1,1,58]{2,1,0:T(1,128)}, u32[]{:S(2)}) copy-start(s32[1,1,58]{2,1,0:T(1,128)} %param.10) | copy-start | bytes 700
  7.2 107.7 %reduce-scatter.3.cloned.1.call-start = ((), (), s32[]{:S(2)}) async-start(), calls=%async_computation.2 | async-start | bytes 81920 | tf_op jit(solution)/shard_map/reduce_scatter | solution.py:52
  95.5 128.4 %reduce-scatter.5.cloned.1.call-start = ((), (), s32[]{:S(2)}) async-start(), calls=%async_computation.3 | async-start | bytes 81920 | tf_op jit(solution)/shard_map/reduce_scatter | solution.py:52
Sparse Core Ops, SparseCore 0:
  95.6 19.2 reduce-scatter.2
  203.6 20.2 reduce-scatter.4
where the time goes:
time: 287 us; the launch traced here: 286 us
  blocking collectives  182 us (63%)
  waiting for transfers between devices  39.7 us (14%)
  matrix products  31.8 us (11%)
  between operations  14.8 us (5%)
  other arithmetic  12.8 us (4%)
  local copies, waits for them, and re-layouts  4.25 us (1%)
    psum x2, blocking collectives, on_device(): lax.psum(local_gram(stacked, stacked), ('row', 'col')) / row_total  79 us
    all_gather x2, blocking collectives, on_device(): gathered = lax.all_gather(vectors, 'row', axis=0, tiled=True)  61.3 us
    psum x1, blocking collectives, on_device(): lax.psum(local_gram(start_block, start_block), ('row', 'col')) / row_total  42 us
    reduce_scatter x2, waiting for transfers between devices, on_device(): lax.psum_scatter(jnp.einsum('rs,ski->rki', selector, operate_product, pre...  39.7 us
    dot_general x2, matrix products, on_device(): jnp.einsum('sij,skj->ski', matrix_tiles, gathered[cols_local], precision=...  16.1 us
    dot_general x22, matrix products, matmul(): jnp.dot(left, right, precision=highest, preferred_element_type=jnp.float32)  8.28 us
  transfers between devices with their start and end apart: 2, of which 2 were waited for; matrix products, arithmetic and copies ran while one was open for 0% of the time, Pallas kernels for 0%

commit v1 on v0

--- a/solution.py
+++ b/solution.py
@@ -39,7 +39,34 @@
     alpha_list = []
     beta_list = []
     for iteration in range(ITERS):
-        gathered = lax.all_gather(vectors, "row", axis=0, tiled=True)
+
+        def find_local_data(piece_in):
+            high, n_now, state_now = (
+                lax.axis_size("row"),
+                lax.axis_index("row"),
+                piece_in.shape[0],
+            )
+            heard = lax.dynamic_update_slice_in_dim(
+                jnp.zeros(
+                    tuple((j0 * high if q == 0 else j0 for q, j0 in enumerate(piece_in.shape))),
+                    piece_in.dtype,
+                ),
+                piece_in,
+                n_now * state_now,
+                axis=0,
+            )
+            for at in [*range(1, high)]:
+                piece_in = lax.ppermute(
+                    piece_in,
+                    axis_name="row",
+                    perm=tuple(((q, (q + 1) % high) for q in range(high))),
+                )
+                heard = lax.dynamic_update_slice_in_dim(
+                    heard, piece_in, (n_now - at) % high * state_now, axis=0
+                )
+            return heard
+
+        gathered = find_local_data(vectors)
         operate_product = jnp.einsum(
             "sij,skj->ski",
             matrix_tiles,

time: 287 us -> 311 us (1.084)
  waiting for transfers between devices: 39.7 us -> 120 us
  blocking collectives: 182 us -> 121 us
  starting transfers between devices: 0.08 us -> 4.74 us
    ppermute x0 -> x14, waiting for transfers between devices: none -> 84.2 us  [find_local_data(): lax.ppermute(piece_in, axis_name='row', perm=tuple(((q, (q + 1) % high) f...]
    all_gather x2 -> x0, blocking collectives: 61.3 us -> none  [on_device(): gathered = lax.all_gather(vectors, 'row', axis=0, tiled=True)]
    ppermute x0 -> x14, starting transfers between devices: none -> 4.66 us  [find_local_data(): lax.ppermute(piece_in, axis_name='row', perm=tuple(((q, (q + 1) % high) f...]
    reduce_scatter x2, waiting for transfers between devices: 39.7 us -> 35.3 us  [on_device(): lax.psum_scatter(jnp.einsum('rs,ski->rki', selector, operate_product, pre...]
  transfers between devices with their start and end apart: 2 -> 16, of which waited for: 2 -> 16; matrix products, arithmetic and copies ran while one was open for 0% -> 0% of each run, Pallas kernels for 0% -> 0%
where the time goes in v1:
time: 311 us; the launch traced here: 310 us
  blocking collectives  121 us (39%)
  waiting for transfers between devices  120 us (39%)
  matrix products  31.8 us (10%)
  between operations  15 us (5%)
  other arithmetic  12.8 us (4%)
  local copies, waits for them, and re-layouts  4.97 us (2%)
  starting transfers between devices  4.74 us (2%)
    ppermute x14, waiting for transfers between devices, find_local_data(): lax.ppermute(piece_in, axis_name='row', perm=tuple(((q, (q + 1) % high) f...  84.2 us
    psum x2, blocking collectives, on_device(): lax.psum(local_gram(stacked, stacked), ('row', 'col')) / row_total  79 us
    psum x1, blocking collectives, on_device(): lax.psum(local_gram(start_block, start_block), ('row', 'col')) / row_total  42 us
    reduce_scatter x2, waiting for transfers between devices, on_device(): lax.psum_scatter(jnp.einsum('rs,ski->rki', selector, operate_product, pre...  35.3 us
    dot_general x2, matrix products, on_device(): jnp.einsum('sij,skj->ski', matrix_tiles, gathered[cols_local], precision=...  16.1 us
    dot_general x22, matrix products, matmul(): jnp.dot(left, right, precision=highest, preferred_element_type=jnp.float32)  8.29 us
  transfers between devices with their start and end apart: 16, of which 16 were waited for; matrix products, arithmetic and copies ran while one was open for 0% of the time, Pallas kernels for 0%

profile of v1, /device:TPU:0, one launch (start us, length us, event | category | flops | bytes accessed | tf_op | source)
XLA Modules:
  0.0 309.8 jit_solution(12107275402540058592)
XLA Ops:
  8.0 42.0 %psum.21 = f32[16,16]{0,1:T(8,128)S(1)} all-reduce(f32[16,16]{0,1:T(8,128)S(1)} %convolution_bitcast_fusion.12), channel_id=1, replica_groups=mesh['row'=8,'col'=4] {'row','col'}, use_global_device_ids=true, to_apply=%region_0.0 | all-reduce | flops 256 | bytes 2048 | tf_op jit(solution)/shard_map/psum | solution.py:31
  54.5 2.3 collective-permute-start
  58.3 2.7 collective-permute-done
  60.9 6.4 %collective-permute-done.1 = f32[2,16,128]{2,1,0:T(8,128)S(1)} collective-permute-done((f32[2,16,128]{2,1,0:T(8,128)S(1)}, f32[2,16,128]{2,1,0:T(8,128)S(1)}, u32[]{:S(2)}, u32[]{:S(2)}) %collective-permute-start.1) | collective-permute-done | bytes 16416 | tf_op jit(solution)/shard_map/ppermute | solution.py:59
  67.4 6.4 %collective-permute-done.2 = f32[2,16,128]{2,1,0:T(8,128)S(1)} collective-permute-done((f32[2,16,128]{2,1,0:T(8,128)S(1)}, f32[2,16,128]{2,1,0:T(8,128)S(1)}, u32[]{:S(2)}, u32[]{:S(2)}) %collective-permute-start.2) | collective-permute-done | bytes 16416 | tf_op jit(solution)/shard_map/ppermute | solution.py:59
  73.8 6.5 %collective-permute-done.3 = f32[2,16,128]{2,1,0:T(8,128)S(1)} collective-permute-done((f32[2,16,128]{2,1,0:T(8,128)S(1)}, f32[2,16,128]{2,1,0:T(8,128)S(1)}, u32[]{:S(2)}, u32[]{:S(2)}) %collective-permute-start.3) | collective-permute-done | bytes 16416 | tf_op jit(solution)/shard_map/ppermute | solution.py:59
  80.3 6.4 %collective-permute-done.4 = f32[2,16,128]{2,1,0:T(8,128)S(1)} collective-permute-done((f32[2,16,128]{2,1,0:T(8,128)S(1)}, f32[2,16,128]{2,1,0:T(8,128)S(1)}, u32[]{:S(2)}, u32[]{:S(2)}) %collective-permute-start.4) | collective-permute-done | bytes 16416 | tf_op jit(solution)/shard_map/ppermute | solution.py:59
  86.8 6.4 %collective-permute-done.5 = f32[2,16,128]{2,1,0:T(8,128)S(1)} collective-permute-done((f32[2,16,128]{2,1,0:T(8,128)S(1)}, f32[2,16,128]{2,1,0:T(8,128)S(1)}, u32[]{:S(2)}, u32[]{:S(2)}) %collective-permute-start.5) | collective-permute-done | bytes 16416 | tf_op jit(solution)/shard_map/ppermute | solution.py:59
  93.2 6.4 %collective-permute-done.6 = f32[2,16,128]{2,1,0:T(8,128)S(1)} collective-permute-done((f32[2,16,128]{2,1,0:T(8,128)S(1)}, f32[2,16,128]{2,1,0:T(8,128)S(1)}, u32[]{:S(2)}, u32[]{:S(2)}) %collective-permute-start.6) | collective-permute-done | bytes 16416 | tf_op jit(solution)/shard_map/ppermute | solution.py:59
  100.2 8.1 %fusion.2 = f32[58,16,128]{2,1,0:T(8,128)S(1)} fusion(f32[58,16,128]{2,1,0:T(8,128)S(1)} %gather_fusion, f32[1,1,58,128,128]{4,3,2,1,0:T(8,128)} %param.9), kind=kOutput, calls=%fused_computation.4 | convolution fusion | flops 182452224 | bytes 4751360 | tf_op jit(solution)/shard_map/sij,skj->ski/dot_general | solution.py:70
  109.4 17.7 %reduce-scatter.3.cloned.1.call-done = f32[2,16,128]{2,1,0:T(8,128)} async-done(((f32[8,16,128]{2,1,0:T(8,128)}), f32[2,16,128]{2,1,0:T(8,128)}) %reduce-scatter.3.cloned.1.call-update) | async-done | bytes 16400 | tf_op jit(solution)/shard_map/reduce_scatter | solution.py:79
  128.1 39.5 %psum.22 = f32[48,48]{0,1:T(8,128)S(1)} all-reduce(f32[48,48]{0,1:T(8,128)S(1)} %convolution_bitcast_fusion.1), channel_id=1, replica_groups=mesh['row'=8,'col'=4] {'row','col'}, use_global_device_ids=true, to_apply=%region_4.7 | all-reduce | flops 2304 | bytes 18432 | tf_op jit(solution)/shard_map/psum | solution.py:92
  169.8 1.5 cholesky.70
  175.3 2.3 collective-permute-start.7
  177.6 4.1 %collective-permute-done.7 = f32[2,16,128]{2,1,0:T(8,128)S(1)} collective-permute-done((f32[2,16,128]{2,1,0:T(8,128)S(1)}, f32[2,16,128]{2,1,0:T(8,128)S(1)}, u32[]{:S(2)}, u32[]{:S(2)}) %collective-permute-start.7) | collective-permute-done | bytes 16416 | tf_op jit(solution)/shard_map/ppermute | solution.py:59
  181.8 6.4 %collective-permute-done.8 = f32[2,16,128]{2,1,0:T(8,128)S(1)} collective-permute-done((f32[2,16,128]{2,1,0:T(8,128)S(1)}, f32[2,16,128]{2,1,0:T(8,128)S(1)}, u32[]{:S(2)}, u32[]{:S(2)}) %collective-permute-start.8) | collective-permute-done | bytes 16416 | tf_op jit(solution)/shard_map/ppermute | solution.py:59
  188.2 6.4 %collective-permute-done.9 = f32[2,16,128]{2,1,0:T(8,128)S(1)} collective-permute-done((f32[2,16,128]{2,1,0:T(8,128)S(1)}, f32[2,16,128]{2,1,0:T(8,128)S(1)}, u32[]{:S(2)}, u32[]{:S(2)}) %collective-permute-start.9) | collective-permute-done | bytes 16416 | tf_op jit(solution)/shard_map/ppermute | solution.py:59
  194.6 6.6 %collective-permute-done.10 = f32[2,16,128]{2,1,0:T(8,128)S(1)} collective-permute-done((f32[2,16,128]{2,1,0:T(8,128)S(1)}, f32[2,16,128]{2,1,0:T(8,128)S(1)}, u32[]{:S(2)}, u32[]{:S(2)}) %collective-permute-start.10) | collective-permute-done | bytes 16416 | tf_op jit(solution)/shard_map/ppermute | solution.py:59
  201.2 6.4 %collective-permute-done.11 = f32[2,16,128]{2,1,0:T(8,128)S(1)} collective-permute-done((f32[2,16,128]{2,1,0:T(8,128)S(1)}, f32[2,16,128]{2,1,0:T(8,128)S(1)}, u32[]{:S(2)}, u32[]{:S(2)}) %collective-permute-start.11) | collective-permute-done | bytes 16416 | tf_op jit(solution)/shard_map/ppermute | solution.py:59
  207.6 6.4 %collective-permute-done.12 = f32[2,16,128]{2,1,0:T(8,128)S(1)} collective-permute-done((f32[2,16,128]{2,1,0:T(8,128)S(1)}, f32[2,16,128]{2,1,0:T(8,128)S(1)}, u32[]{:S(2)}, u32[]{:S(2)}) %collective-permute-start.12) | collective-permute-done | bytes 16416 | tf_op jit(solution)/shard_map/ppermute | solution.py:59
  214.1 6.4 %collective-permute-done.13 = f32[2,16,128]{2,1,0:T(8,128)S(1)} collective-permute-done((f32[2,16,128]{2,1,0:T(8,128)S(1)}, f32[2,16,128]{2,1,0:T(8,128)S(1)}, u32[]{:S(2)}, u32[]{:S(2)}) %collective-permute-start.13) | collective-permute-done | bytes 16416 | tf_op jit(solution)/shard_map/ppermute | solution.py:59
  221.1 8.1 %fusion = f32[58,16,128]{2,1,0:T(8,128)S(1)} fusion(f32[58,16,128]{2,1,0:T(8,128)S(1)} %gather_fusion.1, f32[1,1,58,128,128]{4,3,2,1,0:T(8,128)} %param.9), kind=kOutput, calls=%fused_computation.2 | convolution fusion | flops 182452224 | bytes 4751360 | tf_op jit(solution)/shard_map/sij,skj->ski/dot_general | solution.py:70
  230.3 17.6 %reduce-scatter.5.cloned.1.call-done = f32[2,16,128]{2,1,0:T(8,128)} async-done(((f32[8,16,128]{2,1,0:T(8,128)}), f32[2,16,128]{2,1,0:T(8,128)}) %reduce-scatter.5.cloned.1.call-update) | async-done | bytes 16400 | tf_op jit(solution)/shard_map/reduce_scatter | solution.py:79
  248.9 39.5 %psum.23 = f32[48,48]{0,1:T(8,128)S(1)} all-reduce(f32[48,48]{0,1:T(8,128)S(1)} %convolution_bitcast_fusion), channel_id=1, replica_groups=mesh['row'=8,'col'=4] {'row','col'}, use_global_device_ids=true, to_apply=%region_6.9 | all-reduce | flops 2304 | bytes 18432 | tf_op jit(solution)/shard_map/psum | solution.py:92
  (110 shorter events, 32.1 us)
Async XLA Ops:
  7.2 0.7 copy-start
  7.2 101.1 %copy-start.1 = (s32[1,1,58]{2,1,0:T(1,128)S(1)}, s32[1,1,58]{2,1,0:T(1,128)}, u32[]{:S(2)}) copy-start(s32[1,1,58]{2,1,0:T(1,128)} %param.10) | copy-start | bytes 700
  7.2 119.9 %reduce-scatter.3.cloned.1.call-start = ((), (), s32[]{:S(2)}) async-start(), calls=%async_computation.2 | async-start | bytes 81920 | tf_op jit(solution)/shard_map/reduce_scatter | solution.py:79
  54.5 6.5 %collective-permute-start = (f32[2,16,128]{2,1,0:T(8,128)S(1)}, f32[2,16,128]{2,1,0:T(8,128)S(1)}, u32[]{:S(2)}, u32[]{:S(2)}) collective-permute-start(f32[2,16,128]{2,1,0:T(8,128)S(1)} %get-tuple-element.13), channel_id=1, source_target_pairs={{0,4},{4,8},{8,12},{12,16},{16,20},{20,24},{24,28},{28,0},{1,5},{5... | collective-permute-start | bytes 49160 | tf_op jit(solution)/shard_map/ppermute | solution.py:59
  60.9 6.4 %collective-permute-start.1 = (f32[2,16,128]{2,1,0:T(8,128)S(1)}, f32[2,16,128]{2,1,0:T(8,128)S(1)}, u32[]{:S(2)}, u32[]{:S(2)}) collective-permute-start(f32[2,16,128]{2,1,0:T(8,128)S(1)} %collective-permute-done), channel_id=1, source_target_pairs={{0,4},{4,8},{8,12},{12,16},{16,20},{20,24},{24,28},{28,0},{1,5},{5... | collective-permute-start | bytes 49160 | tf_op jit(solution)/shard_map/ppermute | solution.py:59
  67.4 6.4 %collective-permute-start.2 = (f32[2,16,128]{2,1,0:T(8,128)S(1)}, f32[2,16,128]{2,1,0:T(8,128)S(1)}, u32[]{:S(2)}, u32[]{:S(2)}) collective-permute-start(f32[2,16,128]{2,1,0:T(8,128)S(1)} %collective-permute-done.1), channel_id=1, source_target_pairs={{0,4},{4,8},{8,12},{12,16},{16,20},{20,24},{24,28},{28,0},{1,5},{5... | collective-permute-start | bytes 49160 | tf_op jit(solution)/shard_map/ppermute | solution.py:59
  73.8 6.5 %collective-permute-start.3 = (f32[2,16,128]{2,1,0:T(8,128)S(1)}, f32[2,16,128]{2,1,0:T(8,128)S(1)}, u32[]{:S(2)}, u32[]{:S(2)}) collective-permute-start(f32[2,16,128]{2,1,0:T(8,128)S(1)} %collective-permute-done.2), channel_id=1, source_target_pairs={{0,4},{4,8},{8,12},{12,16},{16,20},{20,24},{24,28},{28,0},{1,5},{5... | collective-permute-start | bytes 49160 | tf_op jit(solution)/shard_map/ppermute | solution.py:59
  80.3 6.4 %collective-permute-start.4 = (f32[2,16,128]{2,1,0:T(8,128)S(1)}, f32[2,16,128]{2,1,0:T(8,128)S(1)}, u32[]{:S(2)}, u32[]{:S(2)}) collective-permute-start(f32[2,16,128]{2,1,0:T(8,128)S(1)} %collective-permute-done.3), channel_id=1, source_target_pairs={{0,4},{4,8},{8,12},{12,16},{16,20},{20,24},{24,28},{28,0},{1,5},{5... | collective-permute-start | bytes 49160 | tf_op jit(solution)/shard_map/ppermute | solution.py:59
  86.7 6.4 %collective-permute-start.5 = (f32[2,16,128]{2,1,0:T(8,128)S(1)}, f32[2,16,128]{2,1,0:T(8,128)S(1)}, u32[]{:S(2)}, u32[]{:S(2)}) collective-permute-start(f32[2,16,128]{2,1,0:T(8,128)S(1)} %collective-permute-done.4), channel_id=1, source_target_pairs={{0,4},{4,8},{8,12},{12,16},{16,20},{20,24},{24,28},{28,0},{1,5},{5... | collective-permute-start | bytes 49160 | tf_op jit(solution)/shard_map/ppermute | solution.py:59
  93.2 6.4 %collective-permute-start.6 = (f32[2,16,128]{2,1,0:T(8,128)S(1)}, f32[2,16,128]{2,1,0:T(8,128)S(1)}, u32[]{:S(2)}, u32[]{:S(2)}) collective-permute-start(f32[2,16,128]{2,1,0:T(8,128)S(1)} %collective-permute-done.5), channel_id=1, source_target_pairs={{0,4},{4,8},{8,12},{12,16},{16,20},{20,24},{24,28},{28,0},{1,5},{5... | collective-permute-start | bytes 49160 | tf_op jit(solution)/shard_map/ppermute | solution.py:59
  109.4 138.6 %reduce-scatter.5.cloned.1.call-start = ((), (), s32[]{:S(2)}) async-start(), calls=%async_computation.3 | async-start | bytes 81920 | tf_op jit(solution)/shard_map/reduce_scatter | solution.py:79
  175.3 6.5 %collective-permute-start.7 = (f32[2,16,128]{2,1,0:T(8,128)S(1)}, f32[2,16,128]{2,1,0:T(8,128)S(1)}, u32[]{:S(2)}, u32[]{:S(2)}) collective-permute-start(f32[2,16,128]{2,1,0:T(8,128)S(1)} %get-tuple-element.15), channel_id=1, source_target_pairs={{0,4},{4,8},{8,12},{12,16},{16,20},{20,24},{24,28},{28,0},{1,5},{5... | collective-permute-start | bytes 49160 | tf_op jit(solution)/shard_map/ppermute | solution.py:59
  181.7 6.4 %collective-permute-start.8 = (f32[2,16,128]{2,1,0:T(8,128)S(1)}, f32[2,16,128]{2,1,0:T(8,128)S(1)}, u32[]{:S(2)}, u32[]{:S(2)}) collective-permute-start(f32[2,16,128]{2,1,0:T(8,128)S(1)} %collective-permute-done.7), channel_id=1, source_target_pairs={{0,4},{4,8},{8,12},{12,16},{16,20},{20,24},{24,28},{28,0},{1,5},{5... | collective-permute-start | bytes 49160 | tf_op jit(solution)/shard_map/ppermute | solution.py:59
  188.2 6.4 %collective-permute-start.9 = (f32[2,16,128]{2,1,0:T(8,128)S(1)}, f32[2,16,128]{2,1,0:T(8,128)S(1)}, u32[]{:S(2)}, u32[]{:S(2)}) collective-permute-start(f32[2,16,128]{2,1,0:T(8,128)S(1)} %collective-permute-done.8), channel_id=1, source_target_pairs={{0,4},{4,8},{8,12},{12,16},{16,20},{20,24},{24,28},{28,0},{1,5},{5... | collective-permute-start | bytes 49160 | tf_op jit(solution)/shard_map/ppermute | solution.py:59
  194.6 6.6 %collective-permute-start.10 = (f32[2,16,128]{2,1,0:T(8,128)S(1)}, f32[2,16,128]{2,1,0:T(8,128)S(1)}, u32[]{:S(2)}, u32[]{:S(2)}) collective-permute-start(f32[2,16,128]{2,1,0:T(8,128)S(1)} %collective-permute-done.9), channel_id=1, source_target_pairs={{0,4},{4,8},{8,12},{12,16},{16,20},{20,24},{24,28},{28,0},{1,5},{5... | collective-permute-start | bytes 49160 | tf_op jit(solution)/shard_map/ppermute | solution.py:59
  201.2 6.4 %collective-permute-start.11 = (f32[2,16,128]{2,1,0:T(8,128)S(1)}, f32[2,16,128]{2,1,0:T(8,128)S(1)}, u32[]{:S(2)}, u32[]{:S(2)}) collective-permute-start(f32[2,16,128]{2,1,0:T(8,128)S(1)} %collective-permute-done.10), channel_id=1, source_target_pairs={{0,4},{4,8},{8,12},{12,16},{16,20},{20,24},{24,28},{28,0},{1,5},{5... | collective-permute-start | bytes 49160 | tf_op jit(solution)/shard_map/ppermute | solution.py:59
  207.6 6.4 %collective-permute-start.12 = (f32[2,16,128]{2,1,0:T(8,128)S(1)}, f32[2,16,128]{2,1,0:T(8,128)S(1)}, u32[]{:S(2)}, u32[]{:S(2)}) collective-permute-start(f32[2,16,128]{2,1,0:T(8,128)S(1)} %collective-permute-done.11), channel_id=1, source_target_pairs={{0,4},{4,8},{8,12},{12,16},{16,20},{20,24},{24,28},{28,0},{1,5},{5... | collective-permute-start | bytes 49160 | tf_op jit(solution)/shard_map/ppermute | solution.py:59
  214.1 6.4 %collective-permute-start.13 = (f32[2,16,128]{2,1,0:T(8,128)S(1)}, f32[2,16,128]{2,1,0:T(8,128)S(1)}, u32[]{:S(2)}, u32[]{:S(2)}) collective-permute-start(f32[2,16,128]{2,1,0:T(8,128)S(1)} %collective-permute-done.12), channel_id=1, source_target_pairs={{0,4},{4,8},{8,12},{12,16},{16,20},{20,24},{24,28},{28,0},{1,5},{5... | collective-permute-start | bytes 49160 | tf_op jit(solution)/shard_map/ppermute | solution.py:59
Sparse Core Ops, SparseCore 0:
  109.5 17.5 reduce-scatter.2
  230.4 17.5 reduce-scatter.4
